TPU v7x, 512 devices: a whole 4x8x8 slice. The times are simulated.
512 devices in a mesh: seq: 16 (over y_hi, z), head: 32 (over x, y_lo, core).
Axes of the slice: x: 4, y: 8 (y_hi: 2, y_lo: 4; y = y_hi * 4 + y_lo), z: 8, core: 2. Of those that a mesh axis runs over, the one named last changes fastest.
Arguments:
- tokens: bfloat16 [16384, 4096], P(('seq', 'head')), may hold values from -6 to 6
- doc_lengths: int32 [16], replicated, may hold values from 1 to 8704, as said below
- value_weight: bfloat16 [4096, 8192], P('seq', 'head'), may hold values from -0.09375 to 0.09375
- gate_weight: bfloat16 [4096, 8192], P('seq', 'head'), may hold values from -0.09375 to 0.09375
- state_weight: bfloat16 [8, 4096, 256], P(None, 'seq'), may hold values from -0.09375 to 0.09375
- step_weight: bfloat16 [4096, 128], P('seq', 'head'), may hold values from -0.09375 to 0.09375
- value_conv: float32 [4, 8192], P(None, 'head'), may hold values from -3 to 3
- state_conv: float32 [8, 4, 256], replicated, may hold values from -3 to 3
- step_bias: float32 [128], P('head'), may hold values from -5 to -3
- log_rate: float32 [128], P('head'), may hold values from -6 to 4
Outputs:
- layer_output: bfloat16 [16384, 8192], P('seq', 'head')
Inputs may be any that keep to these rules, and one draw needn't show every extreme that they name: `doc_lengths`: the 16 documents lie one after another, their lengths sum to 16384, and the last one holds 8704 positions.
All inputs are finite; a program needn't handle non-finite values.
Results may differ from a plain program's by a relative error of at most 0.015.
Values may be sent and summed in bfloat16 or wider, within the bound.
No kernel may reach another device: no remote copies, remote signals or barrier semaphores. Data moves between devices by JAX's collectives and lax.ppermute only.
A program may use at most 64 MiB of HBM per device.

v0:
```python
import jax
import jax.numpy as jnp
from jax import lax
from jax.sharding import Mesh
from jax.sharding import PartitionSpec as P

HEADS = 128
GROUPS = 8
BLOCK = 256
STATE = 128
YH, Z, X, Y, C = (2, 8, 4, 4, 2)
SEQ = ("yh", "z")
HEAD = ("x", "y", "c")
F32 = jnp.float32
BF16 = jnp.bfloat16


def ring(count, step):
    return [(i, (i + step) % count) for i in range(count)]


def along_seq(value, step):
    return lax.ppermute(value, SEQ, [(i, i + step) for i in range(YH * Z - step)])


def ring_gather(block):
    half = block.shape[1] // 2
    right = left = block
    z = lax.axis_index("z")
    held = jnp.zeros((Z,) + block.shape, block.dtype)

    def put(held, piece, offset, row):
        return lax.dynamic_update_slice(held, piece[None], ((z + offset) % Z, 0, row, 0))

    held = put(held, block, 0, 0)
    for step in range(1, 4):
        right = lax.ppermute(right, "z", ring(Z, 1))
        left = lax.ppermute(left, "z", ring(Z, -1))
        held = put(held, right, -step + Z, 0)
        held = put(held, left, step, 0)
    right = lax.ppermute(right[:, :half], "z", ring(Z, 1))
    left = lax.ppermute(left[:, half:], "z", ring(Z, -1))
    held = put(held, right, 4, 0)
    held = put(held, left, 4, half)
    return held


def segment_of(positions, starts):
    reached = (starts[None, :] <= positions[:, None]).astype(jnp.int32)
    return jnp.sum(reached, axis=1) - 1


def causal_conv(extended, taps_weight, seg_ext, row_count):
    tap_count = taps_weight.shape[0]
    own_segment = seg_ext[tap_count - 1 :]
    summed = jnp.zeros((row_count, extended.shape[1]), F32)
    for tap_index in range(tap_count):
        window = extended[tap_index : tap_index + row_count].astype(F32)
        keep_mask = (seg_ext[tap_index : tap_index + row_count] == own_segment).astype(F32)
        summed = summed + taps_weight[tap_index][None, :] * window * keep_mask[:, None]
    return jax.nn.silu(summed).astype(BF16)


def block_terms(b_rows, c_rows, x_rows, decay_rows, step_rows, segments, seg_before):
    block_len = b_rows.shape[0]
    head_total = decay_rows.shape[0]
    x_heads = x_rows.reshape(block_len, head_total, -1)
    cumulative = jnp.cumsum(decay_rows, axis=1)
    products = jnp.dot(c_rows, b_rows.T, preferred_element_type=F32)
    local_index = jnp.arange(block_len)
    allowed = (local_index[None, :] <= local_index[:, None]) & (
        segments[None, :] == segments[:, None]
    )
    spread = cumulative[:, :, None] - cumulative[:, None, :]
    decay_mat = jnp.where(allowed[None], jnp.exp(jnp.where(allowed[None], spread, 0.0)), 0.0)
    scores = (products[None] * decay_mat * step_rows[:, None, :]).astype(BF16)
    y_inner = jnp.einsum("hij,jhp->ihp", scores, x_heads, preferred_element_type=F32)
    ending = cumulative[:, -1]
    trailing = (
        jnp.where((segments == segments[-1])[None, :], jnp.exp(ending[:, None] - cumulative), 0.0)
        * step_rows
    )
    weighted = (trailing.T[:, :, None] * x_heads.astype(F32)).astype(BF16)
    local_state = jnp.dot(b_rows.T, weighted.reshape(block_len, -1), preferred_element_type=F32)
    factor = jnp.where(segments[-1] == seg_before, jnp.exp(ending), 0.0)
    entry_gain = jnp.where((segments == seg_before)[None, :], jnp.exp(cumulative), 0.0)
    return (y_inner.reshape(block_len, -1), local_state, factor, entry_gain)


def spread_heads(values, width):
    return jnp.repeat(values, width, axis=-1)


def scan_shards(state, gain):
    rows = jnp.broadcast_to(gain[None, :], (8, gain.shape[0]))
    packed = jnp.concatenate([state, rows], axis=0)
    near = [along_seq(packed, step) for step in (1, 2, 3)]
    total, gains = (packed[:STATE], packed[STATE : STATE + 1])
    for piece in near:
        total = total + gains * piece[:STATE]
        gains = gains * piece[STATE : STATE + 1]
    packed = jnp.concatenate([total, jnp.broadcast_to(gains, (8, gains.shape[1]))], axis=0)
    first, second = (along_seq(packed, 1), along_seq(packed, 5))
    return first[:STATE] + first[STATE : STATE + 1] * second[:STATE]


def local(
    tokens,
    doc_lengths,
    value_weight,
    gate_weight,
    state_weight,
    step_weight,
    value_conv,
    state_conv,
    step_bias,
    log_rate,
):
    tok_dev = tokens.shape[0] * X * Y * C
    heads_here = step_weight.shape[1]
    tap_count = value_conv.shape[0]
    blocks = tok_dev // BLOCK
    cols = value_weight.shape[1]
    core = lax.axis_index("c")
    group = lax.axis_index("x") * 2 + lax.axis_index("y") // 2
    gathered = lax.all_gather(tokens, HEAD, axis=0, tiled=True)
    state_own = lax.dynamic_index_in_dim(state_weight, group, 0, keepdims=False)
    conv_own = lax.dynamic_index_in_dim(state_conv, group, 0, keepdims=False)
    state_half = jnp.where(core == 0, state_own[:, :STATE], state_own[:, STATE:])
    state_half = jnp.concatenate([state_half[:STATE], state_half[STATE:]], axis=1)
    step_rows = jnp.pad(step_weight.T, ((0, 8 - heads_here), (0, 0)))
    pack = jnp.concatenate([value_weight, state_half, step_rows, gate_weight], axis=0)
    both = lax.all_gather(pack, "yh", axis=0, tiled=False)
    first_rows = 256 + STATE + 8
    gate_all = lax.all_gather(both[:, first_rows:], "z", axis=0, tiled=False)
    held = ring_gather(both[:, :first_rows]).transpose(1, 0, 2, 3)
    depth = tokens.shape[1]
    value_all = held[:, :, :256].reshape(depth, cols)
    state_all = held[:, :, 256 : 256 + STATE]
    state_all = jnp.stack([state_all[..., :STATE], state_all[..., STATE:]], axis=2)
    state_all = state_all.reshape(depth, STATE)
    step_all = held[:, :, 256 + STATE :].transpose(0, 1, 3, 2).reshape(depth, 8)[:, :heads_here]
    half_proj = jnp.dot(gathered, state_all, preferred_element_type=F32).astype(BF16)
    other_proj = lax.ppermute(half_proj, "c", [(0, 1), (1, 0)])
    value_proj = jnp.dot(gathered, value_all, preferred_element_type=F32).astype(BF16)
    step_proj = jnp.dot(gathered, step_all, preferred_element_type=F32).astype(BF16)
    b_proj = jnp.where(core == 0, half_proj, other_proj)
    c_proj = jnp.where(core == 0, other_proj, half_proj)
    state_proj = jnp.concatenate([b_proj, c_proj], axis=1)
    rim_source = jnp.concatenate(
        [value_proj[-(tap_count - 1) :], state_proj[-(tap_count - 1) :]], axis=1
    )
    rim_rows = along_seq(rim_source, 1)
    value_ext = jnp.concatenate([rim_rows[:, :cols], value_proj], axis=0)
    state_ext = jnp.concatenate([rim_rows[:, cols:], state_proj], axis=0)
    starts = jnp.cumsum(doc_lengths) - doc_lengths
    positions = lax.axis_index(SEQ) * tok_dev + jnp.arange(-(tap_count - 1), tok_dev)
    seg_ext = segment_of(positions, starts)
    value_act = causal_conv(value_ext, value_conv, seg_ext, tok_dev)
    state_act = causal_conv(state_ext, conv_own, seg_ext, tok_dev)
    step_size = jax.nn.softplus(step_proj.astype(F32) + step_bias[None, :])
    decay_rate = -jnp.exp(log_rate)[None, :] * step_size
    seg_rows = seg_ext[tap_count - 1 :].reshape(blocks, BLOCK)
    seg_before = seg_ext[tap_count - 2 : tap_count - 2 + tok_dev : BLOCK]
    b_all = state_act[:, :STATE].reshape(blocks, BLOCK, STATE)
    c_all = state_act[:, STATE:].reshape(blocks, BLOCK, STATE)
    x_all = value_act.reshape(blocks, BLOCK, cols)
    decay_all = decay_rate.reshape(blocks, BLOCK, heads_here).transpose(0, 2, 1)
    step_all = step_size.reshape(blocks, BLOCK, heads_here).transpose(0, 2, 1)
    y_inner, local_state, factor, entry_gain = lax.map(
        lambda item: block_terms(*item),
        (b_all, c_all, x_all, decay_all, step_all, seg_rows, seg_before),
    )
    width = cols // heads_here
    factor = spread_heads(factor, width)
    running = jnp.zeros((STATE, cols), F32)
    gain = jnp.ones((cols,), F32)
    inside, gains = ([], [])
    for index in range(blocks):
        inside.append(running)
        gains.append(gain)
        running = factor[index][None, :] * running + local_state[index]
        gain = gain * factor[index]
    entering = scan_shards(running, gain)
    gate_full = gate_all.transpose(1, 0, 2, 3).reshape(depth, cols)
    gate_proj = jnp.dot(gathered, gate_full, preferred_element_type=F32).astype(BF16)
    outs = []
    for index in range(blocks):
        incoming = inside[index] + gains[index][None, :] * entering
        carried = jnp.dot(c_all[index].astype(F32), incoming, precision=lax.Precision.HIGHEST)
        carried = carried * spread_heads(entry_gain[index].T, width)
        total = y_inner[index] + carried + x_all[index].astype(F32)
        gating = jax.nn.silu(gate_proj[index * BLOCK : (index + 1) * BLOCK].astype(F32))
        outs.append((total * gating).astype(BF16))
    return jnp.concatenate(outs, axis=0)


def solution(mesh):
    grid = Mesh(mesh.devices.reshape(YH, Z, X, Y, C), SEQ + HEAD)
    return jax.shard_map(
        local,
        mesh=grid,
        in_specs=(
            P(SEQ + HEAD, None),
            P(),
            P(SEQ, HEAD),
            P(SEQ, HEAD),
            P(None, SEQ, None),
            P(SEQ, HEAD),
            P(None, HEAD),
            P(),
            P(HEAD),
            P(HEAD),
        ),
        out_specs=P(SEQ, HEAD),
        check_vma=False,
    )
```

profile of v0, /device:TPU:112, one launch (start us, length us, event | category | flops | bytes accessed | tf_op | source)
XLA Modules:
  0.0 297.2 jit_solution(12818761446502483740)
XLA Ops:
  6.6 1.2 copy-done
  7.8 1.0 fusion.47
  8.8 21.0 %all-gather = bf16[1296,256]{1,0:T(8,128)(2,1)S(1)} all-gather(bf16[648,256]{1,0:T(8,128)(2,1)S(1)} %fusion.47), channel_id=2, replica_groups=mesh['yh'=2,'z'=8,'x'=4,'y'=4,'c'=2] {'yh'}, dimensions={0}, use_global_device_ids=true | all-gather | bytes 995328 | tf_op jit(solution)/shard_map/all_gather | solution.py:133
  31.4 4.3 %collective-permute-start = (bf16[2,392,256]{2,1,0:T(8,128)(2,1)S(1)}, bf16[2,392,256]{2,1,0:T(8,128)(2,1)S(1)}, u32[]{:S(2)}, u32[]{:S(2)}) collective-permute-start(bf16[2,392,256]{2,1,0:T(8,128)(2,1)S(1)} %slice.371), channel_id=1, source_target_pairs={{0,32},{32,64},{64,96},{96,128},{128,160},{160,192},{192,224},{224... | collective-permute-start | bytes 1204232 | tf_op jit(solution)/shard_map/ppermute | solution.py:37
  35.6 1.9 collective-permute-start.1
  38.4 0.9 constant_dynamic-slice_fusion.5
  39.2 1.9 broadcast_in_dim.172
  41.1 0.8 bitcast_dynamic-update-slice_fusion.6
  42.0 1.4 collective-permute-done
  43.4 4.3 %collective-permute-start.2 = (bf16[2,392,256]{2,1,0:T(8,128)(2,1)S(1)}, bf16[2,392,256]{2,1,0:T(8,128)(2,1)S(1)}, u32[]{:S(2)}, u32[]{:S(2)}) collective-permute-start(bf16[2,392,256]{2,1,0:T(8,128)(2,1)S(1)} %collective-permute-done), channel_id=1, source_target_pairs={{0,32},{32,64},{64,96},{96,128},{128,160},{160,192},{192,224},{224... | collective-permute-start | bytes 1204232 | tf_op jit(solution)/shard_map/ppermute | solution.py:37
  48.1 8.5 %collective-permute-start.3 = (bf16[2,392,256]{2,1,0:T(8,128)(2,1)S(1)}, bf16[2,392,256]{2,1,0:T(8,128)(2,1)S(1)}, u32[]{:S(2)}, u32[]{:S(2)}) collective-permute-start(bf16[2,392,256]{2,1,0:T(8,128)(2,1)S(1)} %collective-permute-done.1), channel_id=1, source_target_pairs={{0,224},{32,0},{64,32},{96,64},{128,96},{160,128},{192,160},{224,1... | collective-permute-start | bytes 1204232 | tf_op jit(solution)/shard_map/ppermute | solution.py:38
  56.6 0.8 bitcast_dynamic-update-slice_fusion.5
  58.1 9.0 %collective-permute-done.2 = bf16[2,392,256]{2,1,0:T(8,128)(2,1)S(1)} collective-permute-done((bf16[2,392,256]{2,1,0:T(8,128)(2,1)S(1)}, bf16[2,392,256]{2,1,0:T(8,128)(2,1)S(1)}, u32[]{:S(2)}, u32[]{:S(2)}) %collective-permute-start.2) | collective-permute-done | bytes 401440 | tf_op jit(solution)/shard_map/ppermute | solution.py:37
  67.2 2.8 collective-permute-start.4
  69.9 1.3 collective-permute-done.3
  71.3 5.5 %collective-permute-start.5 = (bf16[2,392,256]{2,1,0:T(8,128)(2,1)S(1)}, bf16[2,392,256]{2,1,0:T(8,128)(2,1)S(1)}, u32[]{:S(2)}, u32[]{:S(2)}) collective-permute-start(bf16[2,392,256]{2,1,0:T(8,128)(2,1)S(1)} %collective-permute-done.3), channel_id=1, source_target_pairs={{0,224},{32,0},{64,32},{96,64},{128,96},{160,128},{192,160},{224,1... | collective-permute-start | bytes 1204232 | tf_op jit(solution)/shard_map/ppermute | solution.py:38
  76.8 0.8 bitcast_dynamic-update-slice_fusion.3
  77.5 0.8 bitcast_dynamic-update-slice_fusion.2
  78.4 10.5 %collective-permute-done.4 = bf16[2,392,256]{2,1,0:T(8,128)(2,1)S(1)} collective-permute-done((bf16[2,392,256]{2,1,0:T(8,128)(2,1)S(1)}, bf16[2,392,256]{2,1,0:T(8,128)(2,1)S(1)}, u32[]{:S(2)}, u32[]{:S(2)}) %collective-permute-start.4) | collective-permute-done | bytes 401440 | tf_op jit(solution)/shard_map/ppermute | solution.py:37
  88.8 1.9 collective-permute-start.6
  90.8 3.9 %collective-permute-start.7 = (bf16[2,196,256]{2,1,0:T(8,128)(2,1)S(1)}, bf16[2,196,256]{2,1,0:T(8,128)(2,1)S(1)}, u32[]{:S(2)}, u32[]{:S(2)}) collective-permute-start(bf16[2,196,256]{2,1,0:T(8,128)(2,1)S(1)} %slice.373), channel_id=1, source_target_pairs={{0,224},{32,0},{64,32},{96,64},{128,96},{160,128},{192,160},{224,1... | collective-permute-start | bytes 602120 | tf_op jit(solution)/shard_map/ppermute | solution.py:42
  95.5 0.8 bitcast_dynamic-update-slice_fusion
  96.8 2.1 dynamic_update_slice.50
  98.9 1.8 dynamic_update_slice.51
  100.8 3.1 %slice.374 = bf16[2,8,256,256]{3,2,1,0:T(8,128)(2,1)} slice(bf16[2,8,392,256]{3,2,1,0:T(8,128)(2,1)} %bitcast.36), slice={[0:2], [0:8], [0:256], [0:256]} | slice | bytes 4194304 | tf_op jit(solution)/shard_map/slice | solution.py:138
  103.9 0.8 slice.395
  104.7 1.3 slice_bitcast_fusion.1
  106.2 3.2 %copy.121 = bf16[2,8,256,256]{3,2,1,0:T(8,128)(2,1)} copy(bf16[2,8,256,256]{3,2,0,1:T(8,128)(2,1)} %bitcast.241) | data formatting | bytes 4194304 | tf_op jit(solution)/shard_map/transpose | solution.py:185
  109.5 49.4 %all-gather.5.cloned.1.call-done = bf16[1024,4096]{1,0:T(8,128)(2,1)} async-done(((bf16[32,4096]{1,0:T(8,128)(2,1)}), bf16[1024,4096]{1,0:T(8,128)(2,1)}) %all-gather.5.cloned.1.call-update) | async-done | bytes 8388624 | tf_op jit(solution)/shard_map/all_gather | solution.py:126
  158.9 6.4 %fusion.34 = bf16[1024,128]{0,1:T(8,128)(2,1)S(1)} fusion(bf16[4096,128]{1,0:T(8,128)(2,1)S(1)} %bitcast.238, bf16[1024,4096]{1,0:T(8,128)(2,1)} %all-gather.5.cloned.1.call-done), kind=kOutput, calls=%fused_computation.58 | convolution fusion | flops 1073872896 | bytes 9699328 | tf_op jit(solution)/shard_map/dot_general | solution.py:143
  165.3 2.1 collective-permute-start.8
  167.5 4.1 %fusion.20 = bf16[1024,256]{0,1:T(8,128)(2,1)S(1)} fusion(bf16[4096,256]{1,0:T(8,128)(2,1)} %bitcast.242, bf16[1024,4096]{1,0:T(8,128)(2,1)S(1)} %copy-done.1), kind=kOutput, calls=%fused_computation.39 | convolution fusion | flops 2147745792 | bytes 11010048 | tf_op jit(solution)/shard_map/dot_general | solution.py:145
  171.6 3.2 %fusion.21 = bf16[1024,256]{0,1:T(8,128)(2,1)} fusion(bf16[4096,256]{1,0:T(8,128)(2,1)S(1)} %bitcast.243, bf16[1024,4096]{1,0:T(8,128)(2,1)S(1)} %copy-done.1), kind=kOutput, calls=%fused_computation.40 | convolution fusion | flops 2147745792 | bytes 11010048 | tf_op jit(solution)/shard_map/dot_general | solution.py:186
  175.1 3.9 %collective-permute-start.9 = (bf16[3,512]{0,1:T(8,128)(2,1)S(1)}, bf16[3,512]{0,1:T(8,128)(2,1)S(1)}, u32[]{:S(2)}, u32[]{:S(2)}) collective-permute-start(bf16[3,512]{0,1:T(8,128)(2,1)S(1)} %pad_maximum_fusion.6), channel_id=1, source_target_pairs={{0,32},{32,64},{64,96},{96,128},{128,160},{160,192},{192,224},{224... | collective-permute-start | bytes 9224 | tf_op jit(solution)/shard_map/ppermute | solution.py:23
  179.0 2.3 broadcast_multiply_fusion
  181.3 1.3 collective-permute-done.9
  183.0 1.2 multiply_convert_fusion.3
  184.5 1.1 multiply_convert_fusion.4
  185.7 34.4 %while.16 = (s32[]{:T(128)}, f32[4,256,256]{1,2,0:T(8,128)}, f32[4,128,256]{2,1,0:T(8,128)}, f32[4,4]{1,0:T(4,128)S(1)}, f32[4,4,256]{2,1,0:T(4,128)S(1)}, /*ind...) while((s32[]{:T(128)}, f32[4,256,256]{1,2,0:T(8,128)}, ...), condition=%wide.region_5.6_spmd, body=%wide.region_2.5_spmd.sunk | while | flops 69210640 | bytes 2653675 | solution.py:170
  187.0 1.4 compare_reduce_fusion.3
  188.4 1.2 reduce-window.22
  191.9 0.9 fusion.118
  195.6 1.4 compare_reduce_fusion.3
  197.0 1.2 reduce-window.22
  200.5 0.9 fusion.118
  204.2 1.4 compare_reduce_fusion.3
  205.7 1.2 reduce-window.22
  209.1 0.9 fusion.118
  212.8 1.4 compare_reduce_fusion.3
  214.3 1.2 reduce-window.22
  217.7 0.9 fusion.118
  220.7 1.1 bitcast_add_fusion
  221.9 3.7 %collective-permute-start.10 = (f32[136,256]{1,0:T(8,128)S(1)}, f32[136,256]{1,0:T(8,128)S(1)}, u32[]{:S(2)}, u32[]{:S(2)}) collective-permute-start(f32[136,256]{1,0:T(8,128)S(1)} %pad_maximum_fusion.4), channel_id=1, source_target_pairs={{0,32},{32,64},{64,96},{96,128},{128,160},{160,192},{192,224},{224... | collective-permute-start | bytes 417800 | tf_op jit(solution)/shard_map/ppermute | solution.py:23
  225.6 6.9 %collective-permute-start.11 = (f32[136,256]{1,0:T(8,128)S(1)}, f32[136,256]{1,0:T(8,128)S(1)}, u32[]{:S(2)}, u32[]{:S(2)}) collective-permute-start(f32[136,256]{1,0:T(8,128)S(1)} %pad_maximum_fusion.4), channel_id=1, source_target_pairs={{0,64},{32,96},{64,128},{96,160},{128,192},{160,224},{192,256},{22... | collective-permute-start | bytes 417800 | tf_op jit(solution)/shard_map/ppermute | solution.py:23
  232.5 2.0 collective-permute-start.12
  234.7 2.9 collective-permute-done.10
  237.5 24.1 %collective-permute-done.11 = f32[136,256]{1,0:T(8,128)S(1)} collective-permute-done((f32[136,256]{1,0:T(8,128)S(1)}, f32[136,256]{1,0:T(8,128)S(1)}, u32[]{:S(2)}, u32[]{:S(2)}) %collective-permute-start.11) | collective-permute-done | bytes 139296 | tf_op jit(solution)/shard_map/ppermute | solution.py:23
  261.7 2.4 collective-permute-done.12
  264.2 5.1 %collective-permute-start.13 = (f32[136,256]{1,0:T(8,128)S(1)}, f32[136,256]{1,0:T(8,128)S(1)}, u32[]{:S(2)}, u32[]{:S(2)}) collective-permute-start(f32[136,256]{1,0:T(8,128)S(1)} %pad_maximum_fusion.5), channel_id=1, source_target_pairs={{0,32},{32,64},{64,96},{96,128},{128,160},{160,192},{192,224},{224... | collective-permute-start | bytes 417800 | tf_op jit(solution)/shard_map/ppermute | solution.py:23
  269.3 1.9 collective-permute-start.14
  271.3 0.9 collective-permute-done.13
  272.1 14.6 %collective-permute-done.14 = f32[136,256]{1,0:T(8,128)S(1)} collective-permute-done((f32[136,256]{1,0:T(8,128)S(1)}, f32[136,256]{1,0:T(8,128)S(1)}, u32[]{:S(2)}, u32[]{:S(2)}) %collective-permute-start.14) | collective-permute-done | bytes 139296 | tf_op jit(solution)/shard_map/ppermute | solution.py:23
  286.8 1.3 fusion.38
  289.4 1.0 copy.125
  (193 shorter events, 22.6 us)
Async XLA Ops:
  6.5 1.2 copy-start
  6.5 31.0 %copy-start.6 = (s32[16]{0:T(128)S(1)}, s32[16]{0:T(128)}, u32[]{:S(2)}) copy-start(s32[16]{0:T(128)} %param.13) | copy-start | bytes 196
  6.5 31.4 %copy-start.4 = (f32[4,256]{1,0:T(4,128)S(1)}, f32[4,256]{1,0:T(4,128)}, u32[]{:S(2)}) copy-start(f32[4,256]{1,0:T(4,128)} %param.18) | copy-start | bytes 12292
  6.5 31.5 %copy-start.8 = (f32[4]{0:T(128)S(1)}, f32[4]{0:T(128)}, u32[]{:S(2)}) copy-start(f32[4]{0:T(128)} %param.21) | copy-start | bytes 52
  6.5 99.7 %all-gather.7.cloned.1.call-start = ((), (), s32[]{:S(2)}) async-start(), calls=%async_computation.1 | async-start | bytes 2359296 | tf_op jit(solution)/shard_map/all_gather | solution.py:135
  30.6 128.3 %all-gather.5.cloned.1.call-start = ((), (), s32[]{:S(2)}) async-start(), calls=%async_computation | async-start | bytes 8650752 | tf_op jit(solution)/shard_map/all_gather | solution.py:126
  31.4 12.1 %collective-permute-start = (bf16[2,392,256]{2,1,0:T(8,128)(2,1)S(1)}, bf16[2,392,256]{2,1,0:T(8,128)(2,1)S(1)}, u32[]{:S(2)}, u32[]{:S(2)}) collective-permute-start(bf16[2,392,256]{2,1,0:T(8,128)(2,1)S(1)} %slice.371), channel_id=1, source_target_pairs={{0,32},{32,64},{64,96},{96,128},{128,160},{160,192},{192,224},{224... | collective-permute-start | bytes 1204232 | tf_op jit(solution)/shard_map/ppermute | solution.py:37
  35.6 12.4 %collective-permute-start.1 = (bf16[2,392,256]{2,1,0:T(8,128)(2,1)S(1)}, bf16[2,392,256]{2,1,0:T(8,128)(2,1)S(1)}, u32[]{:S(2)}, u32[]{:S(2)}) collective-permute-start(bf16[2,392,256]{2,1,0:T(8,128)(2,1)S(1)} %slice.371), channel_id=1, source_target_pairs={{0,224},{32,0},{64,32},{96,64},{128,96},{160,128},{192,160},{224,1... | collective-permute-start | bytes 1204232 | tf_op jit(solution)/shard_map/ppermute | solution.py:38
  43.4 23.8 %collective-permute-start.2 = (bf16[2,392,256]{2,1,0:T(8,128)(2,1)S(1)}, bf16[2,392,256]{2,1,0:T(8,128)(2,1)S(1)}, u32[]{:S(2)}, u32[]{:S(2)}) collective-permute-start(bf16[2,392,256]{2,1,0:T(8,128)(2,1)S(1)} %collective-permute-done), channel_id=1, source_target_pairs={{0,32},{32,64},{64,96},{96,128},{128,160},{160,192},{192,224},{224... | collective-permute-start | bytes 1204232 | tf_op jit(solution)/shard_map/ppermute | solution.py:37
  48.1 23.2 %collective-permute-start.3 = (bf16[2,392,256]{2,1,0:T(8,128)(2,1)S(1)}, bf16[2,392,256]{2,1,0:T(8,128)(2,1)S(1)}, u32[]{:S(2)}, u32[]{:S(2)}) collective-permute-start(bf16[2,392,256]{2,1,0:T(8,128)(2,1)S(1)} %collective-permute-done.1), channel_id=1, source_target_pairs={{0,224},{32,0},{64,32},{96,64},{128,96},{160,128},{192,160},{224,1... | collective-permute-start | bytes 1204232 | tf_op jit(solution)/shard_map/ppermute | solution.py:38
  67.2 21.6 %collective-permute-start.4 = (bf16[2,392,256]{2,1,0:T(8,128)(2,1)S(1)}, bf16[2,392,256]{2,1,0:T(8,128)(2,1)S(1)}, u32[]{:S(2)}, u32[]{:S(2)}) collective-permute-start(bf16[2,392,256]{2,1,0:T(8,128)(2,1)S(1)} %collective-permute-done.2), channel_id=1, source_target_pairs={{0,32},{32,64},{64,96},{96,128},{128,160},{160,192},{192,224},{224... | collective-permute-start | bytes 1204232 | tf_op jit(solution)/shard_map/ppermute | solution.py:37
  71.3 19.5 %collective-permute-start.5 = (bf16[2,392,256]{2,1,0:T(8,128)(2,1)S(1)}, bf16[2,392,256]{2,1,0:T(8,128)(2,1)S(1)}, u32[]{:S(2)}, u32[]{:S(2)}) collective-permute-start(bf16[2,392,256]{2,1,0:T(8,128)(2,1)S(1)} %collective-permute-done.3), channel_id=1, source_target_pairs={{0,224},{32,0},{64,32},{96,64},{128,96},{160,128},{192,160},{224,1... | collective-permute-start | bytes 1204232 | tf_op jit(solution)/shard_map/ppermute | solution.py:38
  88.8 8.0 %collective-permute-start.6 = (bf16[2,196,256]{2,1,0:T(8,128)(2,1)S(1)}, bf16[2,196,256]{2,1,0:T(8,128)(2,1)S(1)}, u32[]{:S(2)}, u32[]{:S(2)}) collective-permute-start(bf16[2,196,256]{2,1,0:T(8,128)(2,1)S(1)} %slice.372), channel_id=1, source_target_pairs={{0,32},{32,64},{64,96},{96,128},{128,160},{160,192},{192,224},{224... | collective-permute-start | bytes 602120 | tf_op jit(solution)/shard_map/ppermute | solution.py:41
  90.8 8.1 %collective-permute-start.7 = (bf16[2,196,256]{2,1,0:T(8,128)(2,1)S(1)}, bf16[2,196,256]{2,1,0:T(8,128)(2,1)S(1)}, u32[]{:S(2)}, u32[]{:S(2)}) collective-permute-start(bf16[2,196,256]{2,1,0:T(8,128)(2,1)S(1)} %slice.373), channel_id=1, source_target_pairs={{0,224},{32,0},{64,32},{96,64},{128,96},{160,128},{192,160},{224,1... | collective-permute-start | bytes 602120 | tf_op jit(solution)/shard_map/ppermute | solution.py:42
  158.9 8.6 %copy-start.1 = (bf16[1024,4096]{1,0:T(8,128)(2,1)S(1)}, bf16[1024,4096]{1,0:T(8,128)(2,1)}, u32[]{:S(2)}) copy-start(bf16[1024,4096]{1,0:T(8,128)(2,1)} %all-gather.5.cloned.1.call-done) | copy-start | bytes 25165828
  165.3 9.6 %collective-permute-start.8 = (bf16[1024,128]{0,1:T(8,128)(2,1)S(1)}, bf16[1024,128]{0,1:T(8,128)(2,1)S(1)}, u32[]{:S(2)}, u32[]{:S(2)}) collective-permute-start(bf16[1024,128]{0,1:T(8,128)(2,1)S(1)} %fusion.34), channel_id=1, source_target_pairs={{0,1},{1,0},{2,3},{3,2},{4,5},{5,4},{6,7},{7,6},{8,9},{9,8},{10,11... | collective-permute-start | bytes 786440 | tf_op jit(solution)/shard_map/ppermute | solution.py:144
  167.5 4.1 %copy-start.2 = (bf16[2,8,256,256]{3,2,1,0:T(8,128)(2,1)S(1)}, bf16[2,8,256,256]{3,2,1,0:T(8,128)(2,1)}, u32[]{:S(2)}) copy-start(bf16[2,8,256,256]{3,2,1,0:T(8,128)(2,1)} %copy.121) | copy-start | bytes 6291460
  171.6 7.4 %copy-start.5 = (f32[4]{0:T(128)S(1)}, f32[4]{0:T(128)}, u32[]{:S(2)}) copy-start(f32[4]{0:T(128)} %param.20) | copy-start | bytes 52
  175.1 7.6 %collective-permute-start.9 = (bf16[3,512]{0,1:T(8,128)(2,1)S(1)}, bf16[3,512]{0,1:T(8,128)(2,1)S(1)}, u32[]{:S(2)}, u32[]{:S(2)}) collective-permute-start(bf16[3,512]{0,1:T(8,128)(2,1)S(1)} %pad_maximum_fusion.6), channel_id=1, source_target_pairs={{0,32},{32,64},{64,96},{96,128},{128,160},{160,192},{192,224},{224... | collective-permute-start | bytes 9224 | tf_op jit(solution)/shard_map/ppermute | solution.py:23
  220.1 68.1 %copy-start.3 = (f32[4,128,256]{2,1,0:T(8,128)S(1)}, f32[4,128,256]{2,1,0:T(8,128)}, u32[]{:S(2)}) copy-start(f32[4,128,256]{2,1,0:T(8,128)} %get-tuple-element.72) | copy-start | bytes 1572868
  221.9 15.7 %collective-permute-start.10 = (f32[136,256]{1,0:T(8,128)S(1)}, f32[136,256]{1,0:T(8,128)S(1)}, u32[]{:S(2)}, u32[]{:S(2)}) collective-permute-start(f32[136,256]{1,0:T(8,128)S(1)} %pad_maximum_fusion.4), channel_id=1, source_target_pairs={{0,32},{32,64},{64,96},{96,128},{128,160},{160,192},{192,224},{224... | collective-permute-start | bytes 417800 | tf_op jit(solution)/shard_map/ppermute | solution.py:23
  225.6 36.1 %collective-permute-start.11 = (f32[136,256]{1,0:T(8,128)S(1)}, f32[136,256]{1,0:T(8,128)S(1)}, u32[]{:S(2)}, u32[]{:S(2)}) collective-permute-start(f32[136,256]{1,0:T(8,128)S(1)} %pad_maximum_fusion.4), channel_id=1, source_target_pairs={{0,64},{32,96},{64,128},{96,160},{128,192},{160,224},{192,256},{22... | collective-permute-start | bytes 417800 | tf_op jit(solution)/shard_map/ppermute | solution.py:23
  232.5 31.6 %collective-permute-start.12 = (f32[136,256]{1,0:T(8,128)S(1)}, f32[136,256]{1,0:T(8,128)S(1)}, u32[]{:S(2)}, u32[]{:S(2)}) collective-permute-start(f32[136,256]{1,0:T(8,128)S(1)} %pad_maximum_fusion.4), channel_id=1, source_target_pairs={{0,96},{32,128},{64,160},{96,192},{128,224},{160,256},{192,288},{2... | collective-permute-start | bytes 417800 | tf_op jit(solution)/shard_map/ppermute | solution.py:23
  234.7 53.5 %copy-start.7 = (f32[4,256,256]{1,2,0:T(8,128)S(1)}, f32[4,256,256]{1,2,0:T(8,128)}, u32[]{:S(2)}) copy-start(f32[4,256,256]{1,2,0:T(8,128)} %get-tuple-element.70) | copy-start | bytes 3145732
  234.7 53.5 %copy-start.9 = (bf16[1024,256]{0,1:T(8,128)(2,1)S(1)}, bf16[1024,256]{0,1:T(8,128)(2,1)}, u32[]{:S(2)}) copy-start(bf16[1024,256]{0,1:T(8,128)(2,1)} %fusion.21) | copy-start | bytes 1572868
  264.2 7.9 %collective-permute-start.13 = (f32[136,256]{1,0:T(8,128)S(1)}, f32[136,256]{1,0:T(8,128)S(1)}, u32[]{:S(2)}, u32[]{:S(2)}) collective-permute-start(f32[136,256]{1,0:T(8,128)S(1)} %pad_maximum_fusion.5), channel_id=1, source_target_pairs={{0,32},{32,64},{64,96},{96,128},{128,160},{160,192},{192,224},{224... | collective-permute-start | bytes 417800 | tf_op jit(solution)/shard_map/ppermute | solution.py:23
  269.3 17.4 %collective-permute-start.14 = (f32[136,256]{1,0:T(8,128)S(1)}, f32[136,256]{1,0:T(8,128)S(1)}, u32[]{:S(2)}, u32[]{:S(2)}) collective-permute-start(f32[136,256]{1,0:T(8,128)S(1)} %pad_maximum_fusion.5), channel_id=1, source_target_pairs={{0,160},{32,192},{64,224},{96,256},{128,288},{160,320},{192,352},{... | collective-permute-start | bytes 417800 | tf_op jit(solution)/shard_map/ppermute | solution.py:23
Sparse Core Ops, SparseCore 0:
  30.7 56.6 all-gather.6
  89.6 69.2 all-gather.4
where the time goes:
time: 298 us; the launch traced here: 297 us
  waiting for transfers between devices  120 us (40%)
  starting transfers between devices  58.9 us (20%)
  local copies, waits for them, and re-layouts  35.8 us (12%)
  matrix products  24.7 us (8%)
  blocking collectives  21 us (7%)
  other arithmetic  17.4 us (6%)
  between operations  14.1 us (5%)
  loops' own time  5.8 us (2%)
    all_gather x1, waiting for transfers between devices, local(): gathered = lax.all_gather(tokens, HEAD, axis=0, tiled=True)  49.4 us
    ppermute x6, waiting for transfers between devices, along_seq(): lax.ppermute(value, SEQ, [(i, i + step) for i in range(YH * Z - step)])  46.3 us
    ppermute x6, starting transfers between devices, along_seq(): lax.ppermute(value, SEQ, [(i, i + step) for i in range(YH * Z - step)])  23.6 us
    all_gather x1, blocking collectives, local(): both = lax.all_gather(pack, 'yh', axis=0, tiled=False)  21 us
    ppermute x3, waiting for transfers between devices, ring_gather(): right = lax.ppermute(right, 'z', ring(Z, 1))  20.9 us
    ppermute x3, starting transfers between devices, ring_gather(): left = lax.ppermute(left, 'z', ring(Z, -1))  15.9 us
    ppermute x3, starting transfers between devices, ring_gather(): right = lax.ppermute(right, 'z', ring(Z, 1))  11.3 us
    dynamic_update_slice x9, local copies, waits for them, and re-layouts, put(): lax.dynamic_update_slice(held, piece[None], ((z + offset) % Z, 0, row, 0))  9.48 us
  transfers between devices with their start and end apart: 17, of which 13 were waited for; matrix products, arithmetic and copies ran while one was open for 11% of the time, Pallas kernels for 0%

commit v1 on v0

--- a/solution.py
+++ b/solution.py
@@ -123,7 +123,12 @@
     cols = value_weight.shape[1]
     core = lax.axis_index("c")
     group = lax.axis_index("x") * 2 + lax.axis_index("y") // 2
-    gathered = lax.all_gather(tokens, HEAD, axis=0, tiled=True)
+    gathered = jnp.concatenate(
+        lax.all_to_all(
+            jnp.stack(lax.axis_size(HEAD) * [tokens]), axis_name=HEAD, split_axis=0, concat_axis=0
+        ),
+        0,
+    )
     state_own = lax.dynamic_index_in_dim(state_weight, group, 0, keepdims=False)
     conv_own = lax.dynamic_index_in_dim(state_conv, group, 0, keepdims=False)
     state_half = jnp.where(core == 0, state_own[:, :STATE], state_own[:, STATE:])

time: 298 us -> 385 us (1.29)
  the two profiles are of different devices: /device:TPU:112 before, /device:TPU:32 now
where the time goes in v1:
time: 385 us; the launch traced here: 384 us
  blocking collectives  157 us (41%)
  waiting for transfers between devices  67.6 us (18%)
  starting transfers between devices  52.7 us (14%)
  local copies, waits for them, and re-layouts  39.3 us (10%)
  matrix products  33.3 us (9%)
  other arithmetic  15.3 us (4%)
  between operations  14.2 us (4%)
  loops' own time  4.76 us (1%)
    all_gather x1, blocking collectives, local(): both = lax.all_gather(pack, 'yh', axis=0, tiled=False)  157 us
    ppermute x6, waiting for transfers between devices, along_seq(): lax.ppermute(value, SEQ, [(i, i + step) for i in range(YH * Z - step)])  42.1 us
    ppermute x3, waiting for transfers between devices, ring_gather(): right = lax.ppermute(right, 'z', ring(Z, 1))  21.8 us
    ppermute x3, starting transfers between devices, ring_gather(): left = lax.ppermute(left, 'z', ring(Z, -1))  19.7 us
    ppermute x6, starting transfers between devices, along_seq(): lax.ppermute(value, SEQ, [(i, i + step) for i in range(YH * Z - step)])  12.9 us
    dynamic_update_slice x9, local copies, waits for them, and re-layouts, put(): lax.dynamic_update_slice(held, piece[None], ((z + offset) % Z, 0, row, 0))  9.51 us
  transfers between devices with their start and end apart: 17, of which 12 were waited for; matrix products, arithmetic and copies ran while one was open for 11% of the time, Pallas kernels for 0%

profile of v1, /device:TPU:32, one launch (start us, length us, event | category | flops | bytes accessed | tf_op | source)
XLA Modules:
  0.0 384.0 jit_solution(3688036563972074042)
XLA Ops:
  6.5 5.3 %stack.8 = bf16[32,32,4096]{2,1,0:T(8,128)(2,1)} broadcast(bf16[32,4096]{1,0:T(8,128)(2,1)} %param.12), dimensions={1,2} | broadcast | bytes 8650752 | tf_op jit(solution)/shard_map/stack | solution.py:128
  11.8 5.3 %all-to-all-start = ((bf16[32,32,4096]{2,1,0:T(8,128)(2,1)}), bf16[32,32,4096]{2,1,0:T(8,128)(2,1)}, u32[]{:S(2)}, u32[]{:S(2)}) async-start(bf16[32,32,4096]{2,1,0:T(8,128)(2,1)} %stack.8), calls=%async_computation | async-start | bytes 16777216 | tf_op jit(solution)/shard_map/all_to_all | solution.py:127
  17.4 156.9 %all-gather = bf16[1296,256]{1,0:T(8,128)(2,1)S(1)} all-gather(bf16[648,256]{1,0:T(8,128)(2,1)S(1)} %fusion.47), channel_id=2, replica_groups=mesh['yh'=2,'z'=8,'x'=4,'y'=4,'c'=2] {'yh'}, dimensions={0}, use_global_device_ids=true | all-gather | bytes 995328 | tf_op jit(solution)/shard_map/all_gather | solution.py:138
  175.0 1.9 collective-permute-start
  177.0 8.6 %collective-permute-start.1 = (bf16[2,392,256]{2,1,0:T(8,128)(2,1)S(1)}, bf16[2,392,256]{2,1,0:T(8,128)(2,1)S(1)}, u32[]{:S(2)}, u32[]{:S(2)}) collective-permute-start(bf16[2,392,256]{2,1,0:T(8,128)(2,1)S(1)} %slice.371), channel_id=1, source_target_pairs={{0,224},{32,0},{64,32},{96,64},{128,96},{160,128},{192,160},{224,1... | collective-permute-start | bytes 1204232 | tf_op jit(solution)/shard_map/ppermute | solution.py:38
  186.3 0.9 constant_dynamic-slice_fusion.5
  187.2 1.9 broadcast_in_dim.172
  189.9 3.0 collective-permute-done
  192.9 1.9 collective-permute-start.2
  194.8 2.4 collective-permute-done.1
  197.2 5.6 %collective-permute-start.3 = (bf16[2,392,256]{2,1,0:T(8,128)(2,1)S(1)}, bf16[2,392,256]{2,1,0:T(8,128)(2,1)S(1)}, u32[]{:S(2)}, u32[]{:S(2)}) collective-permute-start(bf16[2,392,256]{2,1,0:T(8,128)(2,1)S(1)} %collective-permute-done.1), channel_id=1, source_target_pairs={{0,224},{32,0},{64,32},{96,64},{128,96},{160,128},{192,160},{224,1... | collective-permute-start | bytes 1204232 | tf_op jit(solution)/shard_map/ppermute | solution.py:38
  202.8 0.8 bitcast_dynamic-update-slice_fusion.5
  203.6 0.8 bitcast_dynamic-update-slice_fusion.4
  204.4 11.3 %collective-permute-done.2 = bf16[2,392,256]{2,1,0:T(8,128)(2,1)S(1)} collective-permute-done((bf16[2,392,256]{2,1,0:T(8,128)(2,1)S(1)}, bf16[2,392,256]{2,1,0:T(8,128)(2,1)S(1)}, u32[]{:S(2)}, u32[]{:S(2)}) %collective-permute-start.2) | collective-permute-done | bytes 401440 | tf_op jit(solution)/shard_map/ppermute | solution.py:37
  215.7 1.9 collective-permute-start.4
  218.4 5.6 %collective-permute-start.5 = (bf16[2,392,256]{2,1,0:T(8,128)(2,1)S(1)}, bf16[2,392,256]{2,1,0:T(8,128)(2,1)S(1)}, u32[]{:S(2)}, u32[]{:S(2)}) collective-permute-start(bf16[2,392,256]{2,1,0:T(8,128)(2,1)S(1)} %collective-permute-done.3), channel_id=1, source_target_pairs={{0,224},{32,0},{64,32},{96,64},{128,96},{160,128},{192,160},{224,1... | collective-permute-start | bytes 1204232 | tf_op jit(solution)/shard_map/ppermute | solution.py:38
  224.0 0.8 bitcast_dynamic-update-slice_fusion.3
  224.8 0.8 bitcast_dynamic-update-slice_fusion.2
  225.6 7.5 %collective-permute-done.4 = bf16[2,392,256]{2,1,0:T(8,128)(2,1)S(1)} collective-permute-done((bf16[2,392,256]{2,1,0:T(8,128)(2,1)S(1)}, bf16[2,392,256]{2,1,0:T(8,128)(2,1)S(1)}, u32[]{:S(2)}, u32[]{:S(2)}) %collective-permute-start.4) | collective-permute-done | bytes 401440 | tf_op jit(solution)/shard_map/ppermute | solution.py:37
  233.1 2.1 collective-permute-start.6
  235.2 5.0 %collective-permute-start.7 = (bf16[2,196,256]{2,1,0:T(8,128)(2,1)S(1)}, bf16[2,196,256]{2,1,0:T(8,128)(2,1)S(1)}, u32[]{:S(2)}, u32[]{:S(2)}) collective-permute-start(bf16[2,196,256]{2,1,0:T(8,128)(2,1)S(1)} %slice.373), channel_id=1, source_target_pairs={{0,224},{32,0},{64,32},{96,64},{128,96},{160,128},{192,160},{224,1... | collective-permute-start | bytes 602120 | tf_op jit(solution)/shard_map/ppermute | solution.py:42
  240.2 0.8 bitcast_dynamic-update-slice_fusion.1
  241.0 0.8 bitcast_dynamic-update-slice_fusion
  242.3 2.1 dynamic_update_slice.50
  244.4 1.8 dynamic_update_slice.51
  246.3 3.1 slice.374
  249.4 0.8 slice.395
  250.2 1.3 slice_bitcast_fusion.1
  251.7 3.1 copy.121
  254.9 6.4 %fusion.34 = bf16[1024,128]{0,1:T(8,128)(2,1)S(1)} fusion(bf16[4096,128]{1,0:T(8,128)(2,1)S(1)} %bitcast.239, bf16[1024,4096]{1,0:T(8,128)(2,1)} %bitcast.38), kind=kOutput, calls=%fused_computation.58 | convolution fusion | flops 1073872896 | bytes 9699328 | tf_op jit(solution)/shard_map/dot_general | solution.py:148
  261.3 1.9 collective-permute-start.8
  263.2 5.9 %fusion.20 = bf16[1024,256]{0,1:T(8,128)(2,1)S(1)} fusion(bf16[4096,256]{1,0:T(8,128)(2,1)S(1)} %bitcast.243, bf16[1024,4096]{1,0:T(8,128)(2,1)} %bitcast.38), kind=kOutput, calls=%fused_computation.39 | convolution fusion | flops 2147745792 | bytes 11010048 | tf_op jit(solution)/shard_map/dot_general | solution.py:150
  269.2 6.7 %fusion.21 = bf16[1024,256]{0,1:T(8,128)(2,1)} fusion(bf16[4096,256]{1,0:T(8,128)(2,1)S(1)} %bitcast.244, bf16[1024,4096]{1,0:T(8,128)(2,1)} %bitcast.38), kind=kOutput, calls=%fused_computation.40 | convolution fusion | flops 2147745792 | bytes 11010048 | tf_op jit(solution)/shard_map/dot_general | solution.py:191
  276.1 2.1 collective-permute-start.9
  278.2 5.7 %broadcast_multiply_fusion = (f32[1024,4]{0,1:T(4,128)S(1)}, f32[1024,4]{0,1:T(4,128)S(1)}) fusion(f32[4]{0:T(128)S(1)} %exponential_negate_fusion, f32[4]{0:T(128)S(1)} %copy-done.8, bf16[1024,4096]{1,0:T(8,128)(2,1)} %bitcast.38, bf16[4096,8]{0,1:T(8,128)(2,1)S(1)} %bitcast.247), kind=kOutput, calls=%fused_computation.155 | convolution fusion | flops 33595392 | bytes 8455168 | tf_op jit(solution)/shard_map/dot_general | solution.py:151
  283.9 6.0 %collective-permute-done.9 = bf16[3,512]{0,1:T(8,128)(2,1)S(1)} collective-permute-done((bf16[3,512]{0,1:T(8,128)(2,1)S(1)}, bf16[3,512]{0,1:T(8,128)(2,1)S(1)}, u32[]{:S(2)}, u32[]{:S(2)}) %collective-permute-start.9) | collective-permute-done | bytes 3104 | tf_op jit(solution)/shard_map/ppermute | solution.py:23
  290.2 1.1 multiply_convert_fusion.3
  291.7 1.1 multiply_convert_fusion.4
  292.9 31.6 %while.16 = (s32[]{:T(128)}, f32[4,256,256]{1,2,0:T(8,128)}, f32[4,128,256]{2,1,0:T(8,128)}, f32[4,4]{1,0:T(4,128)S(1)}, f32[4,4,256]{2,1,0:T(4,128)S(1)}, /*ind...) while((s32[]{:T(128)}, f32[4,256,256]{1,2,0:T(8,128)}, ...), condition=%wide.region_5.6_spmd, body=%wide.region_2.5_spmd.sunk | while | flops 69210640 | bytes 2653675 | solution.py:175
  294.1 1.1 compare_reduce_fusion.3
  295.2 1.2 reduce-window.22
  298.7 0.9 fusion.118
  302.0 1.1 compare_reduce_fusion.3
  303.1 1.2 reduce-window.22
  306.6 0.9 fusion.118
  309.9 1.1 compare_reduce_fusion.3
  311.0 1.2 reduce-window.22
  314.6 0.9 fusion.118
  317.8 1.1 compare_reduce_fusion.3
  319.0 1.2 reduce-window.22
  322.5 0.9 fusion.118
  325.2 1.1 bitcast_add_fusion
  326.3 1.9 collective-permute-start.10
  328.3 1.9 collective-permute-start.11
  330.2 3.1 collective-permute-start.12
  333.5 8.4 %collective-permute-done.10 = f32[136,256]{1,0:T(8,128)S(1)} collective-permute-done((f32[136,256]{1,0:T(8,128)S(1)}, f32[136,256]{1,0:T(8,128)S(1)}, u32[]{:S(2)}, u32[]{:S(2)}) %collective-permute-start.10) | collective-permute-done | bytes 139296 | tf_op jit(solution)/shard_map/ppermute | solution.py:23
  341.9 8.1 %collective-permute-done.11 = f32[136,256]{1,0:T(8,128)S(1)} collective-permute-done((f32[136,256]{1,0:T(8,128)S(1)}, f32[136,256]{1,0:T(8,128)S(1)}, u32[]{:S(2)}, u32[]{:S(2)}) %collective-permute-start.11) | collective-permute-done | bytes 139296 | tf_op jit(solution)/shard_map/ppermute | solution.py:23
  350.0 5.0 %collective-permute-done.12 = f32[136,256]{1,0:T(8,128)S(1)} collective-permute-done((f32[136,256]{1,0:T(8,128)S(1)}, f32[136,256]{1,0:T(8,128)S(1)}, u32[]{:S(2)}, u32[]{:S(2)}) %collective-permute-start.12) | collective-permute-done | bytes 139296 | tf_op jit(solution)/shard_map/ppermute | solution.py:23
  355.1 1.9 collective-permute-start.13
  357.0 1.9 collective-permute-start.14
  359.0 9.3 %collective-permute-done.13 = f32[136,256]{1,0:T(8,128)S(1)} collective-permute-done((f32[136,256]{1,0:T(8,128)S(1)}, f32[136,256]{1,0:T(8,128)S(1)}, u32[]{:S(2)}, u32[]{:S(2)}) %collective-permute-start.13) | collective-permute-done | bytes 139296 | tf_op jit(solution)/shard_map/ppermute | solution.py:23
  368.3 5.2 %collective-permute-done.14 = f32[136,256]{1,0:T(8,128)S(1)} collective-permute-done((f32[136,256]{1,0:T(8,128)S(1)}, f32[136,256]{1,0:T(8,128)S(1)}, u32[]{:S(2)}, u32[]{:S(2)}) %collective-permute-start.14) | collective-permute-done | bytes 139296 | tf_op jit(solution)/shard_map/ppermute | solution.py:23
  373.6 1.3 fusion.38
  376.2 1.0 copy.125
  (199 shorter events, 20.8 us)
Async XLA Ops:
  6.5 10.7 %copy-start = (bf16[8,256,256]{2,1,0:T(8,128)(2,1)S(1)}, bf16[8,256,256]{2,1,0:T(8,128)(2,1)}, u32[]{:S(2)}) copy-start(bf16[8,256,256]{2,1,0:T(8,128)(2,1)} %param.16) | copy-start | bytes 3145732
  11.8 5.5 %copy-start.4 = (bf16[256,256]{1,0:T(8,128)(2,1)S(1)}, bf16[256,256]{1,0:T(8,128)(2,1)}, u32[]{:S(2)}) copy-start(bf16[256,256]{1,0:T(8,128)(2,1)} %param.15) | copy-start | bytes 393220
  11.8 5.5 %copy-start.5 = (bf16[256,256]{1,0:T(8,128)(2,1)S(1)}, bf16[256,256]{1,0:T(8,128)(2,1)}, u32[]{:S(2)}) copy-start(bf16[256,256]{1,0:T(8,128)(2,1)} %param.14) | copy-start | bytes 393220
  11.8 5.5 %copy-start.7 = (bf16[256,4]{0,1:T(4,128)(2,1)S(1)}, bf16[256,4]{0,1:T(4,128)(2,1)}, u32[]{:S(2)}) copy-start(bf16[256,4]{0,1:T(4,128)(2,1)} %param.17) | copy-start | bytes 6148
  11.8 243.0 %all-to-all-start = ((bf16[32,32,4096]{2,1,0:T(8,128)(2,1)}), bf16[32,32,4096]{2,1,0:T(8,128)(2,1)}, u32[]{:S(2)}, u32[]{:S(2)}) async-start(bf16[32,32,4096]{2,1,0:T(8,128)(2,1)} %stack.8), calls=%async_computation | async-start | bytes 16777216 | tf_op jit(solution)/shard_map/all_to_all | solution.py:127
  17.1 168.4 %copy-start.9 = (s32[16]{0:T(128)S(1)}, s32[16]{0:T(128)}, u32[]{:S(2)}) copy-start(s32[16]{0:T(128)} %param.13) | copy-start | bytes 196
  17.2 168.8 %copy-start.6 = (f32[4,256]{1,0:T(4,128)S(1)}, f32[4,256]{1,0:T(4,128)}, u32[]{:S(2)}) copy-start(f32[4,256]{1,0:T(4,128)} %param.18) | copy-start | bytes 12292
  17.2 168.9 %copy-start.11 = (f32[4]{0:T(128)S(1)}, f32[4]{0:T(128)}, u32[]{:S(2)}) copy-start(f32[4]{0:T(128)} %param.21) | copy-start | bytes 52
  17.2 234.5 %all-gather.4.cloned.1.call-start = ((), (), s32[]{:S(2)}) async-start(), calls=%async_computation.1 | async-start | bytes 2359296 | tf_op jit(solution)/shard_map/all_gather | solution.py:140
  175.0 17.8 %collective-permute-start = (bf16[2,392,256]{2,1,0:T(8,128)(2,1)S(1)}, bf16[2,392,256]{2,1,0:T(8,128)(2,1)S(1)}, u32[]{:S(2)}, u32[]{:S(2)}) collective-permute-start(bf16[2,392,256]{2,1,0:T(8,128)(2,1)S(1)} %slice.371), channel_id=1, source_target_pairs={{0,32},{32,64},{64,96},{96,128},{128,160},{160,192},{192,224},{224... | collective-permute-start | bytes 1204232 | tf_op jit(solution)/shard_map/ppermute | solution.py:37
  177.0 20.2 %collective-permute-start.1 = (bf16[2,392,256]{2,1,0:T(8,128)(2,1)S(1)}, bf16[2,392,256]{2,1,0:T(8,128)(2,1)S(1)}, u32[]{:S(2)}, u32[]{:S(2)}) collective-permute-start(bf16[2,392,256]{2,1,0:T(8,128)(2,1)S(1)} %slice.371), channel_id=1, source_target_pairs={{0,224},{32,0},{64,32},{96,64},{128,96},{160,128},{192,160},{224,1... | collective-permute-start | bytes 1204232 | tf_op jit(solution)/shard_map/ppermute | solution.py:38
  192.9 22.8 %collective-permute-start.2 = (bf16[2,392,256]{2,1,0:T(8,128)(2,1)S(1)}, bf16[2,392,256]{2,1,0:T(8,128)(2,1)S(1)}, u32[]{:S(2)}, u32[]{:S(2)}) collective-permute-start(bf16[2,392,256]{2,1,0:T(8,128)(2,1)S(1)} %collective-permute-done), channel_id=1, source_target_pairs={{0,32},{32,64},{64,96},{96,128},{128,160},{160,192},{192,224},{224... | collective-permute-start | bytes 1204232 | tf_op jit(solution)/shard_map/ppermute | solution.py:37
  197.2 21.2 %collective-permute-start.3 = (bf16[2,392,256]{2,1,0:T(8,128)(2,1)S(1)}, bf16[2,392,256]{2,1,0:T(8,128)(2,1)S(1)}, u32[]{:S(2)}, u32[]{:S(2)}) collective-permute-start(bf16[2,392,256]{2,1,0:T(8,128)(2,1)S(1)} %collective-permute-done.1), channel_id=1, source_target_pairs={{0,224},{32,0},{64,32},{96,64},{128,96},{160,128},{192,160},{224,1... | collective-permute-start | bytes 1204232 | tf_op jit(solution)/shard_map/ppermute | solution.py:38
  215.7 17.4 %collective-permute-start.4 = (bf16[2,392,256]{2,1,0:T(8,128)(2,1)S(1)}, bf16[2,392,256]{2,1,0:T(8,128)(2,1)S(1)}, u32[]{:S(2)}, u32[]{:S(2)}) collective-permute-start(bf16[2,392,256]{2,1,0:T(8,128)(2,1)S(1)} %collective-permute-done.2), channel_id=1, source_target_pairs={{0,32},{32,64},{64,96},{96,128},{128,160},{160,192},{192,224},{224... | collective-permute-start | bytes 1204232 | tf_op jit(solution)/shard_map/ppermute | solution.py:37
  218.4 16.8 %collective-permute-start.5 = (bf16[2,392,256]{2,1,0:T(8,128)(2,1)S(1)}, bf16[2,392,256]{2,1,0:T(8,128)(2,1)S(1)}, u32[]{:S(2)}, u32[]{:S(2)}) collective-permute-start(bf16[2,392,256]{2,1,0:T(8,128)(2,1)S(1)} %collective-permute-done.3), channel_id=1, source_target_pairs={{0,224},{32,0},{64,32},{96,64},{128,96},{160,128},{192,160},{224,1... | collective-permute-start | bytes 1204232 | tf_op jit(solution)/shard_map/ppermute | solution.py:38
  233.1 9.2 %collective-permute-start.6 = (bf16[2,196,256]{2,1,0:T(8,128)(2,1)S(1)}, bf16[2,196,256]{2,1,0:T(8,128)(2,1)S(1)}, u32[]{:S(2)}, u32[]{:S(2)}) collective-permute-start(bf16[2,196,256]{2,1,0:T(8,128)(2,1)S(1)} %slice.372), channel_id=1, source_target_pairs={{0,32},{32,64},{64,96},{96,128},{128,160},{160,192},{192,224},{224... | collective-permute-start | bytes 602120 | tf_op jit(solution)/shard_map/ppermute | solution.py:41
  235.2 9.2 %collective-permute-start.7 = (bf16[2,196,256]{2,1,0:T(8,128)(2,1)S(1)}, bf16[2,196,256]{2,1,0:T(8,128)(2,1)S(1)}, u32[]{:S(2)}, u32[]{:S(2)}) collective-permute-start(bf16[2,196,256]{2,1,0:T(8,128)(2,1)S(1)} %slice.373), channel_id=1, source_target_pairs={{0,224},{32,0},{64,32},{96,64},{128,96},{160,128},{192,160},{224,1... | collective-permute-start | bytes 602120 | tf_op jit(solution)/shard_map/ppermute | solution.py:42
  254.9 8.4 %copy-start.1 = (bf16[2,8,256,256]{3,2,1,0:T(8,128)(2,1)S(1)}, bf16[2,8,256,256]{3,2,1,0:T(8,128)(2,1)}, u32[]{:S(2)}) copy-start(bf16[2,8,256,256]{3,2,1,0:T(8,128)(2,1)} %slice.374) | copy-start | bytes 6291460
  261.3 14.6 %collective-permute-start.8 = (bf16[1024,128]{0,1:T(8,128)(2,1)S(1)}, bf16[1024,128]{0,1:T(8,128)(2,1)S(1)}, u32[]{:S(2)}, u32[]{:S(2)}) collective-permute-start(bf16[1024,128]{0,1:T(8,128)(2,1)S(1)} %fusion.34), channel_id=1, source_target_pairs={{0,1},{1,0},{2,3},{3,2},{4,5},{5,4},{6,7},{7,6},{8,9},{9,8},{10,11... | collective-permute-start | bytes 786440 | tf_op jit(solution)/shard_map/ppermute | solution.py:149
  263.2 5.9 %copy-start.2 = (bf16[2,8,256,256]{3,2,1,0:T(8,128)(2,1)S(1)}, bf16[2,8,256,256]{3,2,1,0:T(8,128)(2,1)}, u32[]{:S(2)}) copy-start(bf16[2,8,256,256]{3,2,1,0:T(8,128)(2,1)} %copy.121) | copy-start | bytes 6291460
  269.2 9.1 %copy-start.8 = (f32[4]{0:T(128)S(1)}, f32[4]{0:T(128)}, u32[]{:S(2)}) copy-start(f32[4]{0:T(128)} %param.20) | copy-start | bytes 52
  276.1 13.8 %collective-permute-start.9 = (bf16[3,512]{0,1:T(8,128)(2,1)S(1)}, bf16[3,512]{0,1:T(8,128)(2,1)S(1)}, u32[]{:S(2)}, u32[]{:S(2)}) collective-permute-start(bf16[3,512]{0,1:T(8,128)(2,1)S(1)} %pad_maximum_fusion.6), channel_id=1, source_target_pairs={{0,32},{32,64},{64,96},{96,128},{128,160},{160,192},{192,224},{224... | collective-permute-start | bytes 9224 | tf_op jit(solution)/shard_map/ppermute | solution.py:23
  324.5 50.4 %copy-start.3 = (f32[4,128,256]{2,1,0:T(8,128)S(1)}, f32[4,128,256]{2,1,0:T(8,128)}, u32[]{:S(2)}) copy-start(f32[4,128,256]{2,1,0:T(8,128)} %get-tuple-element.72) | copy-start | bytes 1572868
  326.3 15.6 %collective-permute-start.10 = (f32[136,256]{1,0:T(8,128)S(1)}, f32[136,256]{1,0:T(8,128)S(1)}, u32[]{:S(2)}, u32[]{:S(2)}) collective-permute-start(f32[136,256]{1,0:T(8,128)S(1)} %pad_maximum_fusion.4), channel_id=1, source_target_pairs={{0,32},{32,64},{64,96},{96,128},{128,160},{160,192},{192,224},{224... | collective-permute-start | bytes 417800 | tf_op jit(solution)/shard_map/ppermute | solution.py:23
  328.3 21.7 %collective-permute-start.11 = (f32[136,256]{1,0:T(8,128)S(1)}, f32[136,256]{1,0:T(8,128)S(1)}, u32[]{:S(2)}, u32[]{:S(2)}) collective-permute-start(f32[136,256]{1,0:T(8,128)S(1)} %pad_maximum_fusion.4), channel_id=1, source_target_pairs={{0,64},{32,96},{64,128},{96,160},{128,192},{160,224},{192,256},{22... | collective-permute-start | bytes 417800 | tf_op jit(solution)/shard_map/ppermute | solution.py:23
  330.2 24.8 %collective-permute-start.12 = (f32[136,256]{1,0:T(8,128)S(1)}, f32[136,256]{1,0:T(8,128)S(1)}, u32[]{:S(2)}, u32[]{:S(2)}) collective-permute-start(f32[136,256]{1,0:T(8,128)S(1)} %pad_maximum_fusion.4), channel_id=1, source_target_pairs={{0,96},{32,128},{64,160},{96,192},{128,224},{160,256},{192,288},{2... | collective-permute-start | bytes 417800 | tf_op jit(solution)/shard_map/ppermute | solution.py:23
  333.5 41.4 %copy-start.10 = (f32[4,256,256]{1,2,0:T(8,128)S(1)}, f32[4,256,256]{1,2,0:T(8,128)}, u32[]{:S(2)}) copy-start(f32[4,256,256]{1,2,0:T(8,128)} %get-tuple-element.70) | copy-start | bytes 3145732
  333.5 41.4 %copy-start.12 = (bf16[1024,256]{0,1:T(8,128)(2,1)S(1)}, bf16[1024,256]{0,1:T(8,128)(2,1)}, u32[]{:S(2)}) copy-start(bf16[1024,256]{0,1:T(8,128)(2,1)} %fusion.21) | copy-start | bytes 1572868
  355.1 13.2 %collective-permute-start.13 = (f32[136,256]{1,0:T(8,128)S(1)}, f32[136,256]{1,0:T(8,128)S(1)}, u32[]{:S(2)}, u32[]{:S(2)}) collective-permute-start(f32[136,256]{1,0:T(8,128)S(1)} %pad_maximum_fusion.5), channel_id=1, source_target_pairs={{0,32},{32,64},{64,96},{96,128},{128,160},{160,192},{192,224},{224... | collective-permute-start | bytes 417800 | tf_op jit(solution)/shard_map/ppermute | solution.py:23
  357.0 16.5 %collective-permute-start.14 = (f32[136,256]{1,0:T(8,128)S(1)}, f32[136,256]{1,0:T(8,128)S(1)}, u32[]{:S(2)}, u32[]{:S(2)}) collective-permute-start(f32[136,256]{1,0:T(8,128)S(1)} %pad_maximum_fusion.5), channel_id=1, source_target_pairs={{0,160},{32,192},{64,224},{96,256},{128,288},{160,320},{192,352},{... | collective-permute-start | bytes 417800 | tf_op jit(solution)/shard_map/ppermute | solution.py:23
Sparse Core Ops, SparseCore 0:
  175.1 55.0 all-gather.3
